TPU v7x, 32 devices: a whole 2x2x4 slice. The times are simulated.
32 devices in a mesh: wide: 16 (over z, y, core), narrow: 2 (over x).
Axes of the slice: x: 2, y: 2, z: 4, core: 2. Of those that a mesh axis runs over, the one named last changes fastest.
Arguments:
- concentrations: float32 [256, 32, 256], P('wide', 'narrow'), may hold values from 0.1 to 2
- wind_speeds: bfloat16 [2, 2, 32, 256], P(None, None, ('narrow', 'wide')), may hold values from -0.59765625 to 0.59765625
- rate_constants: float32 [768], replicated, may hold values from 0.05 to 1
- reactants: int32 [768, 2], replicated, may hold values from 0 to 255
- products: int32 [768, 2], replicated, may hold values from 0 to 255
Outputs:
- after_chemistry: float32 [256, 32, 256], P(None, ('narrow', 'wide'))
Inputs may be any that keep to these rules, and one draw needn't show every extreme that they name: `reactants`: each entry is a species number. `products`: each entry is a species number.
All inputs are finite; a program needn't handle non-finite values.
Results may differ from a plain program's by a relative error of at most 0.0003.
Values may be sent and summed in bfloat16 or wider, within the bound.
A program may use at most 64 MiB of HBM per device.

v0:
```python
import jax
import jax.numpy as jnp
from jax import lax
from jax.sharding import PartitionSpec as P

S = 256
SUB = 2
SECTIONS = 6
DIFFUSION = 0.1
CHEM_STEP = 0.02


def padded(cells, sides, width):
    for axis, dim in sides:
        count = lax.axis_size(axis)
        head = lax.slice_in_dim(cells, 0, width, axis=dim)
        tail = lax.slice_in_dim(cells, cells.shape[dim] - width, cells.shape[dim], axis=dim)
        cells = jnp.concatenate(
            [
                lax.ppermute(tail, axis, [(i, (i + 1) % count) for i in range(count)]),
                cells,
                lax.ppermute(head, axis, [((i + 1) % count, i) for i in range(count)]),
            ],
            axis=dim,
        )
    return cells


def take_range(array, begin_at, end_at, along):
    along = along % array.ndim
    index = [slice(None)] * array.ndim
    index[along] = slice(begin_at, end_at)
    return array[tuple(index)]


def minmod(first_jump, second_jump):
    return jnp.maximum(0.0, jnp.minimum(first_jump, second_jump)) + jnp.minimum(
        0.0, jnp.maximum(first_jump, second_jump)
    )


def sweep_axis(extended, speeds, along, closed):
    length = extended.shape[along]
    speed_face = 0.5 * (
        take_range(speeds, 0, length - 1, along) + take_range(speeds, 1, length, along)
    )
    jumps = take_range(extended, 1, length, along) - take_range(extended, 0, length - 1, along)
    slopes = minmod(
        take_range(jumps, 0, length - 2, along), take_range(jumps, 1, length - 1, along)
    )
    inner_speed = take_range(speed_face, 1, length - 2, along)
    left_value = take_range(extended, 1, length - 2, along) + 0.5 * (
        1.0 - inner_speed
    ) * take_range(slopes, 0, length - 3, along)
    right_value = take_range(extended, 2, length - 1, along) - 0.5 * (
        1.0 + inner_speed
    ) * take_range(slopes, 1, length - 2, along)
    face_flux = inner_speed * jnp.where(
        inner_speed >= 0.0, left_value, right_value
    ) - DIFFUSION * take_range(jumps, 1, length - 2, along)
    if closed:
        position = lax.broadcasted_iota(jnp.int32, face_flux.shape, along % face_flux.ndim)
        face_flux = jnp.where((position > 0) & (position < length - 4), face_flux, 0.0)
    return take_range(extended, 2, length - 2, along) - (
        take_range(face_flux, 1, length - 3, along) - take_range(face_flux, 0, length - 4, along)
    )


def sweep_second(tracer, speeds):
    pad_tracer = [(0, 0)] * (tracer.ndim - 1) + [(2, 2)]
    pad_speeds = [(0, 0)] * (speeds.ndim - 1) + [(2, 2)]
    return sweep_axis(
        jnp.pad(tracer, pad_tracer, mode="edge"), jnp.pad(speeds, pad_speeds, mode="edge"), -1, True
    )


def react_cells(cell_block, rate_constants, first_ids, second_ids, net_matrix):
    for section_index in range(SECTIONS):
        rate_values = (
            rate_constants[:, None]
            * jnp.take(cell_block, first_ids, axis=0)
            * jnp.take(cell_block, second_ids, axis=0)
        )
        cell_block = cell_block + CHEM_STEP * jnp.dot(
            net_matrix, rate_values, precision=lax.Precision.HIGHEST
        )
    return cell_block


def on_device(concentrations, wind_speeds, rate_constants, reactants, products):
    groups = concentrations.shape[0]
    row_count = wind_speeds.shape[2]
    columns = wind_speeds.shape[3]
    wide_count = lax.axis_size("wide")
    planes = wind_speeds.reshape(SUB * 2, row_count, columns)
    gathered = lax.all_gather(planes, "wide", axis=1, tiled=True).astype(jnp.float32)
    tracer = concentrations
    stacked = jnp.concatenate([tracer, gathered], 0)
    extended = padded(stacked, (("narrow", 1),), 4)
    wind_rims = extended[groups:]
    tracer = sweep_axis(extended[:groups], wind_rims[0], -2, False)
    tracer = sweep_second(tracer, wind_rims[1, 2:-2])
    tracer = sweep_axis(tracer, wind_rims[2, 2:-2], -2, False)
    tracer = sweep_second(tracer, wind_rims[3, 4:-4])
    species_ids = lax.broadcasted_iota(jnp.int32, (S, rate_constants.shape[0]), 0)

    def one_hot(species_column):
        return (species_ids == species_column[None, :]).astype(jnp.float32)

    net_matrix = (
        one_hot(products[:, 0])
        + one_hot(products[:, 1])
        - one_hot(reactants[:, 0])
        - one_hot(reactants[:, 1])
    )
    first_ids = reactants[:, 0]
    second_ids = reactants[:, 1]
    shaped = tracer.reshape(groups, wide_count, row_count, columns)
    cell_block = lax.all_to_all(shaped, "wide", split_axis=1, concat_axis=0, tiled=True)
    flattened = cell_block.reshape(cell_block.shape[0], -1)
    regrouped = react_cells(flattened, rate_constants, first_ids, second_ids, net_matrix).reshape(
        cell_block.shape
    )
    return regrouped.reshape(S, row_count, columns)


def solution(mesh):
    return jax.shard_map(
        on_device,
        mesh=mesh,
        in_specs=(
            P("wide", "narrow", None),
            P(None, None, ("narrow", "wide"), None),
            P(),
            P(),
            P(),
        ),
        out_specs=P(None, ("narrow", "wide"), None),
        check_vma=False,
    )
```

profile of v0, /device:TPU:0, one launch (start us, length us, event | category | flops | bytes accessed | tf_op | source)
XLA Modules:
  0.0 136.4 jit_solution(5072353564964290958)
XLA Ops:
  0.7 23.2 %all_gather.3 = bf16[4,16,256]{2,0,1:T(4,128)(2,1)S(1)} all-gather(bf16[4,1,256]{2,0,1:T(4,128)(2,1)S(1)} %reshape.84), channel_id=1, replica_groups=mesh['wide'=16,'narrow'=2] {'wide'}, dimensions={1}, use_global_device_ids=true | all-gather | bytes 34816 | tf_op jit(solution)/shard_map/all_gather | solution.py:96
  38.3 2.5 %copy.88 = f32[16,23,256]{1,0,2:T(8,128)} copy(f32[16,23,256]{2,1,0:T(8,128)S(1)} %get-tuple-element.29) | data formatting | bytes 753664
  40.8 2.5 %copy.89 = f32[16,23,256]{1,0,2:T(8,128)} copy(f32[16,23,256]{2,1,0:T(8,128)S(1)} %get-tuple-element.28) | data formatting | bytes 753664
  43.2 2.5 %sub.79 = f32[16,23,256]{1,0,2:T(8,128)S(1)} subtract(f32[16,23,256]{1,0,2:T(8,128)} %copy.88, f32[16,23,256]{1,0,2:T(8,128)} %copy.89) | non-fusion elementwise | flops 94208 | bytes 1130496 | tf_op jit(solution)/shard_map/sub | solution.py:47
  47.6 2.5 %copy.87 = f32[16,21,256]{1,0,2:T(8,128)} copy(f32[16,21,256]{2,1,0:T(8,128)S(1)} %get-tuple-element.26) | data formatting | bytes 688128
  50.1 2.5 %copy.90 = f32[16,21,256]{1,0,2:T(8,128)} copy(f32[16,21,256]{2,1,0:T(8,128)S(1)} %get-tuple-element.27) | data formatting | bytes 688128
  54.4 2.5 %copy.86 = f32[16,20,256]{1,0,2:T(8,128)} copy(f32[16,20,256]{2,1,0:T(8,128)S(1)} %slice.393) | data formatting | bytes 655360
  56.9 4.8 %fusion.22 = f32[16,21,256]{1,0,2:T(8,128)S(1)} fusion(f32[16,23,256]{1,0,2:T(8,128)S(1)} %sub.79, f32[16,21,256]{1,0,2:T(8,128)} %copy.90, f32[16,22,256]{1,0,2:T(8,128)} %minimum_add_fusion.3, f32[16,21,256]{1,0,2:T(8,128)} %copy.87, f32[21,256]{0,1:T(8,128)S(1)} %copy.70, f32[21,256]{0,1:T(8,128)S(1)} %copy.66, f32[21,256]{0,1:T(8,128)S(1)} %copy-done.7, ...), kind=kLoop, calls=%fused_computation.59 | loop fusion | flops 688128 | bytes 2134272 | tf_op jit(solution)/shard_map/sub | solution.py:58
  65.9 6.3 %fusion.7 = f32[16,20,257]{1,0,2:T(8,128)S(1)} fusion(f32[16,20,259]{1,0,2:T(8,128)S(1)} %slice_subtract_fusion.1, f32[16,20,258]{1,0,2:T(8,128)} %minimum_add_fusion.1, f32[16,20,2]{1,0,2:T(8,128)S(1)} %reshape.88, f32[16,20,256]{1,0,2:T(8,128)} %copy-done, f32[16,20,2]{1,0,2:T(8,128)S(1)} %reshape.87, f32[20,257]{0,1:T(8,128)S(1)} %copy.74, ...), kind=kLoop, calls=%fused_computation.31 | loop fusion | flops 904640 | bytes 1715717 | tf_op jit(solution)/shard_map/jit(_where)/select_n | solution.py:63
  75.5 5.1 %fusion.15 = f32[16,17,256]{1,0,2:T(8,128)S(1)} fusion(f32[16,19,256]{1,0,2:T(8,128)} %copy-done.2, f32[16,18,256]{1,0,2:T(8,128)} %minimum_add_fusion.2, f32[16,20,256]{1,0,2:T(8,128)S(1)} %fusion.20, f32[17,256]{0,1:T(8,128)S(1)} %copy.78, f32[17,256]{0,1:T(8,128)S(1)} %copy.77, f32[17,256]{0,1:T(8,128)S(1)} %copy-done.6, pred[17,256]{0,1:T(8,128)(4,1)S(1)} %copy.76), kind=kLoop, calls=%fused_computation.46 | loop fusion | flops 557056 | bytes 1727744 | tf_op jit(solution)/shard_map/sub | solution.py:58
  83.0 2.8 %fusion.1 = f32[16,16,257]{1,0,2:T(8,128)S(1)} fusion(f32[16,16,259]{1,0,2:T(8,128)S(1)} %slice_subtract_fusion, f32[16,16,258]{1,0,2:T(8,128)S(1)} %minimum_add_fusion, f32[16,16,2]{1,0,2:T(8,128)S(1)} %reshape.92, f32[16,16,256]{1,0,2:T(8,128)S(1)} %fusion.14, f32[16,16,2]{1,0,2:T(8,128)S(1)} %reshape.91, f32[16,257]{0,1:T(8,128)S(1)} %copy-done.4, ...), kind=kLoop, calls=%fused_computation.20 | loop fusion | flops 723712 | bytes 1372625 | tf_op jit(solution)/shard_map/jit(_where)/select_n | solution.py:63
  88.0 3.8 %all-to-all-start = ((f32[16,16,1,256]{3,0,2,1:T(8,128)}), f32[16,16,1,256]{3,0,2,1:T(8,128)S(1)}, u32[]{:S(2)}, u32[]{:S(2)}) async-start(f32[16,16,1,256]{3,0,2,1:T(8,128)} %copy.83), calls=%async_computation | async-start | bytes 524288 | tf_op jit(solution)/shard_map/all_to_all | solution.py:119
  91.9 9.7 %all-to-all-done = f32[16,16,1,256]{3,0,2,1:T(8,128)S(1)} async-done(((f32[16,16,1,256]{3,0,2,1:T(8,128)}), f32[16,16,1,256]{3,0,2,1:T(8,128)S(1)}, u32[]{:S(2)}, u32[]{:S(2)}) %all-to-all-start) | async-done | bytes 262176 | tf_op jit(solution)/shard_map/all_to_all | solution.py:119
  103.6 2.1 %gather_fusion.1 = f32[768,256]{1,0:T(8,128)S(1)} fusion(f32[256,256]{1,0:T(8,128)S(1)} %bitcast.31, s32[1024]{0:T(1024)S(1)} %pad_clamp_fusion), kind=kCustom, calls=%fused_computation.1.clone | custom fusion | bytes 1575936 | tf_op jit(solution)/shard_map/jit(_take)/gather | solution.py:82
  107.1 2.1 %gather_fusion.2 = f32[768,256]{1,0:T(8,128)S(1)} fusion(f32[256,256]{1,0:T(8,128)S(1)} %fusion.32, s32[1024]{0:T(1024)S(1)} %pad_clamp_fusion.1), kind=kCustom, calls=%fused_computation.2.clone | custom fusion | bytes 1575936 | tf_op jit(solution)/shard_map/jit(_take)/gather | solution.py:81
  109.3 2.1 %gather_fusion.3 = f32[768,256]{1,0:T(8,128)S(1)} fusion(f32[256,256]{1,0:T(8,128)S(1)} %fusion.32, s32[1024]{0:T(1024)S(1)} %pad_clamp_fusion), kind=kCustom, calls=%fused_computation.3.clone | custom fusion | bytes 1575936 | tf_op jit(solution)/shard_map/jit(_take)/gather | solution.py:82
  112.7 2.1 %gather_fusion.4 = f32[768,256]{1,0:T(8,128)S(1)} fusion(f32[256,256]{1,0:T(8,128)S(1)} %fusion.31, s32[1024]{0:T(1024)S(1)} %pad_clamp_fusion.1), kind=kCustom, calls=%fused_computation.4.clone | custom fusion | bytes 1575936 | tf_op jit(solution)/shard_map/jit(_take)/gather | solution.py:81
  114.9 2.1 %gather_fusion.5 = f32[768,256]{1,0:T(8,128)S(1)} fusion(f32[256,256]{1,0:T(8,128)S(1)} %fusion.31, s32[1024]{0:T(1024)S(1)} %pad_clamp_fusion), kind=kCustom, calls=%fused_computation.5.clone | custom fusion | bytes 1575936 | tf_op jit(solution)/shard_map/jit(_take)/gather | solution.py:82
  118.4 2.1 %gather_fusion.6 = f32[768,256]{1,0:T(8,128)S(1)} fusion(f32[256,256]{1,0:T(8,128)S(1)} %fusion.30, s32[1024]{0:T(1024)S(1)} %pad_clamp_fusion.1), kind=kCustom, calls=%fused_computation.6.clone | custom fusion | bytes 1575936 | tf_op jit(solution)/shard_map/jit(_take)/gather | solution.py:81
  120.5 2.1 %gather_fusion.7 = f32[768,256]{1,0:T(8,128)S(1)} fusion(f32[256,256]{1,0:T(8,128)S(1)} %fusion.30, s32[1024]{0:T(1024)S(1)} %pad_clamp_fusion), kind=kCustom, calls=%fused_computation.7.clone | custom fusion | bytes 1575936 | tf_op jit(solution)/shard_map/jit(_take)/gather | solution.py:82
  124.0 2.1 %gather_fusion.8 = f32[768,256]{1,0:T(8,128)S(1)} fusion(f32[256,256]{1,0:T(8,128)S(1)} %fusion.29, s32[1024]{0:T(1024)S(1)} %pad_clamp_fusion.1), kind=kCustom, calls=%fused_computation.8.clone | custom fusion | bytes 1575936 | tf_op jit(solution)/shard_map/jit(_take)/gather | solution.py:81
  126.1 2.4 %gather_fusion.9 = f32[768,256]{1,0:T(8,128)S(1)} fusion(f32[256,256]{1,0:T(8,128)S(1)} %fusion.29, s32[1024]{0:T(1024)S(1)} %pad_clamp_fusion), kind=kCustom, calls=%fused_computation.9.clone | custom fusion | bytes 1575936 | tf_op jit(solution)/shard_map/jit(_take)/gather | solution.py:82
  129.8 2.1 %gather_fusion.10 = f32[768,256]{1,0:T(8,128)S(1)} fusion(f32[256,256]{1,0:T(8,128)S(1)} %fusion.28, s32[1024]{0:T(1024)S(1)} %pad_clamp_fusion.1), kind=kCustom, calls=%fused_computation.10.clone | custom fusion | bytes 1575936 | tf_op jit(solution)/shard_map/jit(_take)/gather | solution.py:81
  131.9 2.1 %gather_fusion.11 = f32[768,256]{1,0:T(8,128)S(1)} fusion(f32[256,256]{1,0:T(8,128)S(1)} %fusion.28, s32[1024]{0:T(1024)S(1)} %pad_clamp_fusion), kind=kCustom, calls=%fused_computation.11.clone | custom fusion | bytes 1575936 | tf_op jit(solution)/shard_map/jit(_take)/gather | solution.py:82
  (127 shorter events, 41.8 us)
Async XLA Ops:
  24.9 6.4 %collective-permute-start = (f32[20,4,256]{2,1,0:T(4,128)S(1)}, f32[20,4,256]{2,1,0:T(4,128)S(1)}, u32[]{:S(2)}, u32[]{:S(2)}) collective-permute-start(f32[20,4,256]{2,1,0:T(4,128)S(1)} %get-tuple-element.30), channel_id=1, source_target_pairs={{0,1},{1,0},{2,3},{3,2},{4,5},{5,4},{6,7},{7,6},{8,9},{9,8},{10,11... | collective-permute-start | bytes 245768 | tf_op jit(solution)/shard_map/ppermute | solution.py:20
  26.5 5.0 %collective-permute-start.1 = (f32[20,4,256]{2,1,0:T(4,128)S(1)}, f32[20,4,256]{2,1,0:T(4,128)S(1)}, u32[]{:S(2)}, u32[]{:S(2)}) collective-permute-start(f32[20,4,256]{2,1,0:T(4,128)S(1)} %get-tuple-element.31), channel_id=1, source_target_pairs={{1,0},{0,1},{3,2},{2,3},{5,4},{4,5},{7,6},{6,7},{9,8},{8,9},{11,10... | collective-permute-start | bytes 245768 | tf_op jit(solution)/shard_map/ppermute | solution.py:22
  50.1 2.5 %copy-start.13 = (f32[21,256]{1,0:T(8,128)S(1)}, f32[21,256]{1,0:T(8,128)}, u32[]{:S(2)}) copy-start(f32[21,256]{1,0:T(8,128)} %get-tuple-element.42) | copy-start | bytes 64516
  50.1 6.8 %copy-start.7 = (f32[21,256]{0,1:T(8,128)S(1)}, f32[21,256]{0,1:T(8,128)}, u32[]{:S(2)}) copy-start(f32[21,256]{0,1:T(8,128)} %copy.63) | copy-start | bytes 64516
  56.9 4.8 %copy-start.3 = (f32[16,20,256]{1,0,2:T(8,128)S(1)}, f32[16,20,256]{1,0,2:T(8,128)}, u32[]{:S(2)}) copy-start(f32[16,20,256]{1,0,2:T(8,128)} %copy.86) | copy-start | bytes 983044
  62.3 1.3 copy-start
  63.8 1.7 %copy-start.9 = (f32[20,257]{1,0:T(8,128)S(1)}, f32[20,257]{1,0:T(8,128)}, u32[]{:S(2)}) copy-start(f32[20,257]{1,0:T(8,128)} %get-tuple-element.32) | copy-start | bytes 61684
  63.8 1.8 %copy-start.8 = (f32[20,257]{1,0:T(8,128)S(1)}, f32[20,257]{1,0:T(8,128)}, u32[]{:S(2)}) copy-start(f32[20,257]{1,0:T(8,128)} %get-tuple-element.33) | copy-start | bytes 61684
  63.8 1.9 %copy-start.14 = (pred[20,257]{1,0:T(8,128)(4,1)S(1)}, pred[20,257]{1,0:T(8,128)(4,1)}, u32[]{:S(2)}) copy-start(pred[20,257]{1,0:T(8,128)(4,1)} %get-tuple-element.18) | copy-start | bytes 15424
  63.8 2.1 %copy-start.5 = (f32[20,257]{0,1:T(8,128)S(1)}, f32[20,257]{0,1:T(8,128)}, u32[]{:S(2)}) copy-start(f32[20,257]{0,1:T(8,128)} %copy.71) | copy-start | bytes 61684
  63.8 2.1 %copy-start.19 = (pred[257]{0:T(512)(128)(4,1)S(1)}, pred[257]{0:T(512)(128)(4,1)}, u32[]{:S(2)}) copy-start(pred[257]{0:T(512)(128)(4,1)} %fusion.90) | copy-start | bytes 775
  65.9 6.4 %copy-start.1 = (f32[16,20,256]{1,0,2:T(8,128)S(1)}, f32[16,20,256]{1,0,2:T(8,128)}, u32[]{:S(2)}) copy-start(f32[16,20,256]{1,0,2:T(8,128)} %copy-done) | copy-start | bytes 983044
  73.1 2.0 %copy-start.2 = (f32[16,19,256]{1,0,2:T(8,128)}, f32[16,19,256]{1,0,2:T(8,128)S(1)}, u32[]{:S(2)}) copy-start(f32[16,19,256]{1,0,2:T(8,128)S(1)} %slice_subtract_fusion.4) | copy-start | bytes 933892
  73.2 2.0 %copy-start.12 = (f32[17,256]{1,0:T(8,128)S(1)}, f32[17,256]{1,0:T(8,128)}, u32[]{:S(2)}) copy-start(f32[17,256]{1,0:T(8,128)} %get-tuple-element.40) | copy-start | bytes 52228
  73.2 2.1 %copy-start.11 = (f32[17,256]{1,0:T(8,128)S(1)}, f32[17,256]{1,0:T(8,128)}, u32[]{:S(2)}) copy-start(f32[17,256]{1,0:T(8,128)} %get-tuple-element.41) | copy-start | bytes 52228
  73.2 2.2 %copy-start.15 = (pred[17,256]{1,0:T(8,128)(4,1)S(1)}, pred[17,256]{1,0:T(8,128)(4,1)}, u32[]{:S(2)}) copy-start(pred[17,256]{1,0:T(8,128)(4,1)} %get-tuple-element.16) | copy-start | bytes 13060
  73.2 2.3 %copy-start.6 = (f32[17,256]{0,1:T(8,128)S(1)}, f32[17,256]{0,1:T(8,128)}, u32[]{:S(2)}) copy-start(f32[17,256]{0,1:T(8,128)} %copy.75) | copy-start | bytes 52228
  82.1 0.9 copy-start.4
  82.1 0.9 copy-start.10
  86.2 5.6 %copy-start.17 = (s32[768]{0:T(1024)S(1)}, s32[768]{0:T(1024)}, u32[]{:S(2)}) copy-start(s32[768]{0:T(1024)} %get-tuple-element.45) | copy-start | bytes 9220
  86.2 5.6 %copy-start.16 = (s32[768]{0:T(1024)S(1)}, s32[768]{0:T(1024)}, u32[]{:S(2)}) copy-start(s32[768]{0:T(1024)} %get-tuple-element.44) | copy-start | bytes 9220
  86.2 5.6 %copy-start.18 = (s32[768,2]{0,1:T(2,128)S(1)}, s32[768,2]{0,1:T(2,128)}, u32[]{:S(2)}) copy-start(s32[768,2]{0,1:T(2,128)} %param.11) | copy-start | bytes 18436
  88.0 13.5 %all-to-all-start = ((f32[16,16,1,256]{3,0,2,1:T(8,128)}), f32[16,16,1,256]{3,0,2,1:T(8,128)S(1)}, u32[]{:S(2)}, u32[]{:S(2)}) async-start(f32[16,16,1,256]{3,0,2,1:T(8,128)} %copy.83), calls=%async_computation | async-start | bytes 524288 | tf_op jit(solution)/shard_map/all_to_all | solution.py:119
  103.6 2.1 %copy-start.20 = (f32[768]{0:T(1024)S(1)}, f32[768]{0:T(1024)}, u32[]{:S(2)}) copy-start(f32[768]{0:T(1024)} %param.9) | copy-start | bytes 9220
where the time goes:
time: 137 us; the launch traced here: 136 us
  local copies, waits for them, and re-layouts  52.4 us (38%)
  other arithmetic  36.3 us (26%)
  blocking collectives  23.2 us (17%)
  waiting for transfers between devices  9.79 us (7%)
  matrix products  8.2 us (6%)
  starting transfers between devices  5.84 us (4%)
    all_gather x1, blocking collectives, on_device(): lax.all_gather(planes, 'wide', axis=1, tiled=True).astype(jnp.float32)  23.2 us
    unnamed x49, local copies, waits for them, and re-layouts  15.1 us
    gather x6, local copies, waits for them, and re-layouts, react_cells(): jnp.take(cell_block, second_ids, axis=0)  12.9 us
    gather x6, local copies, waits for them, and re-layouts, react_cells(): jnp.take(cell_block, first_ids, axis=0)  12.6 us
    sub x2, other arithmetic, sweep_axis(): inner_speed * jnp.where(inner_speed >= 0.0, left_value, right_value)  9.84 us
    all_to_all x1, waiting for transfers between devices, on_device(): lax.all_to_all(shaped, 'wide', split_axis=1, concat_axis=0, tiled=True)  9.66 us
    select_n x2, other arithmetic, sweep_axis(): jnp.where((position > 0) & (position < length - 4), face_flux, 0.0)  9.12 us
    dot_general x6, matrix products, react_cells(): jnp.dot(net_matrix, rate_values, precision=lax.Precision.HIGHEST)  8.2 us
  transfers between devices with their start and end apart: 3, of which 2 were waited for; matrix products, arithmetic and copies ran while one was open for 3% of the time, Pallas kernels for 0%

commit v1 on v0

--- a/solution.py
+++ b/solution.py
@@ -8,6 +8,11 @@
 SECTIONS = 6
 DIFFUSION = 0.1
 CHEM_STEP = 0.02
+
+
+def gather_over(shard, axis, dim):
+    outgoing = jnp.stack([shard] * lax.axis_size(axis))
+    return jnp.concatenate(lax.all_to_all(outgoing, axis, 0, 0), axis=dim)
 
 
 def padded(cells, sides, width):
@@ -93,7 +98,7 @@
     columns = wind_speeds.shape[3]
     wide_count = lax.axis_size("wide")
     planes = wind_speeds.reshape(SUB * 2, row_count, columns)
-    gathered = lax.all_gather(planes, "wide", axis=1, tiled=True).astype(jnp.float32)
+    gathered = gather_over(planes, "wide", 1).astype(jnp.float32)
     tracer = concentrations
     stacked = jnp.concatenate([tracer, gathered], 0)
     extended = padded(stacked, (("narrow", 1),), 4)

time: 137 us -> 127 us (0.927)
  blocking collectives: 23.2 us -> 0 us
  starting transfers between devices: 5.84 us -> 13.3 us
  waiting for transfers between devices: 9.79 us -> 15.1 us
    all_gather x1 -> x0, blocking collectives: 23.2 us -> none  [on_device(): lax.all_gather(planes, 'wide', axis=1, tiled=True).astype(jnp.float32)]
    all_to_all x0 -> x1, starting transfers between devices: none -> 7.41 us  [gather_over(): return jnp.concatenate(lax.all_to_all(outgoing, axis, 0, 0), axis=dim)]
    all_to_all x0 -> x1, waiting for transfers between devices: none -> 3.7 us  [gather_over(): return jnp.concatenate(lax.all_to_all(outgoing, axis, 0, 0), axis=dim)]
  transfers between devices with their start and end apart: 3 -> 4, of which waited for: 2 -> 4; matrix products, arithmetic and copies ran while one was open for 3% -> 4% of each run, Pallas kernels for 0% -> 0%
where the time goes in v1:
time: 127 us
  local copies, waits for them, and re-layouts  53.1 us (42%)
  other arithmetic  36.2 us (29%)
  waiting for transfers between devices  15.1 us (12%)
  starting transfers between devices  13.3 us (10%)
  matrix products  8.2 us (6%)
    unnamed x49, local copies, waits for them, and re-layouts  15.2 us
    gather x6, local copies, waits for them, and re-layouts, react_cells(): jnp.take(cell_block, second_ids, axis=0)  12.9 us
    gather x6, local copies, waits for them, and re-layouts, react_cells(): jnp.take(cell_block, first_ids, axis=0)  12.6 us
    sub x2, other arithmetic, sweep_axis(): inner_speed * jnp.where(inner_speed >= 0.0, left_value, right_value)  9.84 us
    all_to_all x1, waiting for transfers between devices, on_device(): lax.all_to_all(shaped, 'wide', split_axis=1, concat_axis=0, tiled=True)  9.66 us
    select_n x2, other arithmetic, sweep_axis(): jnp.where((position > 0) & (position < length - 4), face_flux, 0.0)  9.11 us
    dot_general x6, matrix products, react_cells(): jnp.dot(net_matrix, rate_values, precision=lax.Precision.HIGHEST)  8.2 us
    all_to_all x1, starting transfers between devices, gather_over(): return jnp.concatenate(lax.all_to_all(outgoing, axis, 0, 0), axis=dim)  7.41 us
  transfers between devices with their start and end apart: 4, of which 4 were waited for; matrix products, arithmetic and copies ran while one was open for 4% of the time, Pallas kernels for 0%

profile of v1, /device:TPU:0, one launch (start us, length us, event | category | flops | bytes accessed | tf_op | source)
XLA Modules:
  0.0 126.7 jit_solution(13693207859035510798)
XLA Ops:
  1.3 7.4 %all-to-all-start = ((bf16[16,4,1,256]{3,1,2,0:T(4,128)(2,1)}), bf16[16,4,1,256]{3,1,2,0:T(4,128)(2,1)S(1)}, u32[]{:S(2)}, u32[]{:S(2)}) async-start(bf16[16,4,1,256]{3,1,2,0:T(4,128)(2,1)} %stack.3), calls=%async_computation | async-start | bytes 65536 | tf_op jit(solution)/shard_map/all_to_all | solution.py:15
  11.7 3.7 %all-to-all-done = bf16[16,4,1,256]{3,1,2,0:T(4,128)(2,1)S(1)} async-done(((bf16[16,4,1,256]{3,1,2,0:T(4,128)(2,1)}), bf16[16,4,1,256]{3,1,2,0:T(4,128)(2,1)S(1)}, u32[]{:S(2)}, u32[]{:S(2)}) %all-to-all-start) | async-done | bytes 32800 | tf_op jit(solution)/shard_map/all_to_all | solution.py:15
  28.5 2.5 %copy.79 = f32[16,23,256]{1,0,2:T(8,128)} copy(f32[16,23,256]{2,1,0:T(8,128)S(1)} %get-tuple-element.29) | data formatting | bytes 753664
  31.0 2.5 %copy.80 = f32[16,23,256]{1,0,2:T(8,128)} copy(f32[16,23,256]{2,1,0:T(8,128)S(1)} %get-tuple-element.28) | data formatting | bytes 753664
  33.4 2.5 %sub.79 = f32[16,23,256]{1,0,2:T(8,128)S(1)} subtract(f32[16,23,256]{1,0,2:T(8,128)} %copy.79, f32[16,23,256]{1,0,2:T(8,128)} %copy.80) | non-fusion elementwise | flops 94208 | bytes 1130496 | tf_op jit(solution)/shard_map/sub | solution.py:52
  37.8 2.5 %copy.78 = f32[16,21,256]{1,0,2:T(8,128)} copy(f32[16,21,256]{2,1,0:T(8,128)S(1)} %get-tuple-element.26) | data formatting | bytes 688128
  40.4 2.5 %copy.81 = f32[16,21,256]{1,0,2:T(8,128)} copy(f32[16,21,256]{2,1,0:T(8,128)S(1)} %get-tuple-element.27) | data formatting | bytes 688128
  44.6 2.5 %copy.77 = f32[16,20,256]{1,0,2:T(8,128)} copy(f32[16,20,256]{2,1,0:T(8,128)S(1)} %slice.394) | data formatting | bytes 655360
  47.2 4.8 %fusion.22 = f32[16,21,256]{1,0,2:T(8,128)S(1)} fusion(f32[16,23,256]{1,0,2:T(8,128)S(1)} %sub.79, f32[16,21,256]{1,0,2:T(8,128)} %copy.81, f32[16,22,256]{1,0,2:T(8,128)} %minimum_add_fusion.3, f32[16,21,256]{1,0,2:T(8,128)} %copy.78, f32[21,256]{0,1:T(8,128)S(1)} %copy.61, f32[21,256]{0,1:T(8,128)S(1)} %copy.57, f32[21,256]{0,1:T(8,128)S(1)} %copy-done.7, ...), kind=kLoop, calls=%fused_computation.59 | loop fusion | flops 688128 | bytes 2134272 | tf_op jit(solution)/shard_map/sub | solution.py:63
  56.1 6.3 %fusion.7 = f32[16,20,257]{1,0,2:T(8,128)S(1)} fusion(f32[16,20,259]{1,0,2:T(8,128)S(1)} %slice_subtract_fusion.1, f32[16,20,258]{1,0,2:T(8,128)} %minimum_add_fusion.1, f32[16,20,2]{1,0,2:T(8,128)S(1)} %reshape.93, f32[16,20,256]{1,0,2:T(8,128)} %copy-done, f32[16,20,2]{1,0,2:T(8,128)S(1)} %reshape.92, f32[20,257]{0,1:T(8,128)S(1)} %copy.65, ...), kind=kLoop, calls=%fused_computation.31 | loop fusion | flops 904640 | bytes 1715717 | tf_op jit(solution)/shard_map/jit(_where)/select_n | solution.py:68
  65.7 5.1 %fusion.15 = f32[16,17,256]{1,0,2:T(8,128)S(1)} fusion(f32[16,19,256]{1,0,2:T(8,128)} %copy-done.2, f32[16,18,256]{1,0,2:T(8,128)} %minimum_add_fusion.2, f32[16,20,256]{1,0,2:T(8,128)S(1)} %fusion.20, f32[17,256]{0,1:T(8,128)S(1)} %copy.69, f32[17,256]{0,1:T(8,128)S(1)} %copy.68, f32[17,256]{0,1:T(8,128)S(1)} %copy-done.6, pred[17,256]{0,1:T(8,128)(4,1)S(1)} %copy.67), kind=kLoop, calls=%fused_computation.46 | loop fusion | flops 557056 | bytes 1727744 | tf_op jit(solution)/shard_map/sub | solution.py:63
  73.2 2.8 %fusion.1 = f32[16,16,257]{1,0,2:T(8,128)S(1)} fusion(f32[16,16,259]{1,0,2:T(8,128)S(1)} %slice_subtract_fusion, f32[16,16,258]{1,0,2:T(8,128)S(1)} %minimum_add_fusion, f32[16,16,2]{1,0,2:T(8,128)S(1)} %reshape.97, f32[16,16,256]{1,0,2:T(8,128)S(1)} %fusion.14, f32[16,16,2]{1,0,2:T(8,128)S(1)} %reshape.96, f32[16,257]{0,1:T(8,128)S(1)} %copy-done.4, ...), kind=kLoop, calls=%fused_computation.20 | loop fusion | flops 723712 | bytes 1372625 | tf_op jit(solution)/shard_map/jit(_where)/select_n | solution.py:68
  78.2 3.8 %all-to-all-start.1 = ((f32[16,16,1,256]{3,0,2,1:T(8,128)}), f32[16,16,1,256]{3,0,2,1:T(8,128)S(1)}, u32[]{:S(2)}, u32[]{:S(2)}) async-start(f32[16,16,1,256]{3,0,2,1:T(8,128)} %copy.74), calls=%async_computation.1 | async-start | bytes 524288 | tf_op jit(solution)/shard_map/all_to_all | solution.py:124
  82.1 9.7 %all-to-all-done.1 = f32[16,16,1,256]{3,0,2,1:T(8,128)S(1)} async-done(((f32[16,16,1,256]{3,0,2,1:T(8,128)}), f32[16,16,1,256]{3,0,2,1:T(8,128)S(1)}, u32[]{:S(2)}, u32[]{:S(2)}) %all-to-all-start.1) | async-done | bytes 262176 | tf_op jit(solution)/shard_map/all_to_all | solution.py:124
  93.9 2.1 %gather_fusion.1 = f32[768,256]{1,0:T(8,128)S(1)} fusion(f32[256,256]{1,0:T(8,128)S(1)} %bitcast.36, s32[1024]{0:T(1024)S(1)} %pad_clamp_fusion), kind=kCustom, calls=%fused_computation.1.clone | custom fusion | bytes 1575936 | tf_op jit(solution)/shard_map/jit(_take)/gather | solution.py:87
  97.4 2.1 %gather_fusion.2 = f32[768,256]{1,0:T(8,128)S(1)} fusion(f32[256,256]{1,0:T(8,128)S(1)} %fusion.32, s32[1024]{0:T(1024)S(1)} %pad_clamp_fusion.1), kind=kCustom, calls=%fused_computation.2.clone | custom fusion | bytes 1575936 | tf_op jit(solution)/shard_map/jit(_take)/gather | solution.py:86
  99.5 2.1 %gather_fusion.3 = f32[768,256]{1,0:T(8,128)S(1)} fusion(f32[256,256]{1,0:T(8,128)S(1)} %fusion.32, s32[1024]{0:T(1024)S(1)} %pad_clamp_fusion), kind=kCustom, calls=%fused_computation.3.clone | custom fusion | bytes 1575936 | tf_op jit(solution)/shard_map/jit(_take)/gather | solution.py:87
  103.0 2.1 %gather_fusion.4 = f32[768,256]{1,0:T(8,128)S(1)} fusion(f32[256,256]{1,0:T(8,128)S(1)} %fusion.31, s32[1024]{0:T(1024)S(1)} %pad_clamp_fusion.1), kind=kCustom, calls=%fused_computation.4.clone | custom fusion | bytes 1575936 | tf_op jit(solution)/shard_map/jit(_take)/gather | solution.py:86
  105.1 2.1 %gather_fusion.5 = f32[768,256]{1,0:T(8,128)S(1)} fusion(f32[256,256]{1,0:T(8,128)S(1)} %fusion.31, s32[1024]{0:T(1024)S(1)} %pad_clamp_fusion), kind=kCustom, calls=%fused_computation.5.clone | custom fusion | bytes 1575936 | tf_op jit(solution)/shard_map/jit(_take)/gather | solution.py:87
  108.6 2.1 %gather_fusion.6 = f32[768,256]{1,0:T(8,128)S(1)} fusion(f32[256,256]{1,0:T(8,128)S(1)} %fusion.30, s32[1024]{0:T(1024)S(1)} %pad_clamp_fusion.1), kind=kCustom, calls=%fused_computation.6.clone | custom fusion | bytes 1575936 | tf_op jit(solution)/shard_map/jit(_take)/gather | solution.py:86
  110.7 2.1 %gather_fusion.7 = f32[768,256]{1,0:T(8,128)S(1)} fusion(f32[256,256]{1,0:T(8,128)S(1)} %fusion.30, s32[1024]{0:T(1024)S(1)} %pad_clamp_fusion), kind=kCustom, calls=%fused_computation.7.clone | custom fusion | bytes 1575936 | tf_op jit(solution)/shard_map/jit(_take)/gather | solution.py:87
  114.2 2.1 %gather_fusion.8 = f32[768,256]{1,0:T(8,128)S(1)} fusion(f32[256,256]{1,0:T(8,128)S(1)} %fusion.29, s32[1024]{0:T(1024)S(1)} %pad_clamp_fusion.1), kind=kCustom, calls=%fused_computation.8.clone | custom fusion | bytes 1575936 | tf_op jit(solution)/shard_map/jit(_take)/gather | solution.py:86
  116.3 2.4 %gather_fusion.9 = f32[768,256]{1,0:T(8,128)S(1)} fusion(f32[256,256]{1,0:T(8,128)S(1)} %fusion.29, s32[1024]{0:T(1024)S(1)} %pad_clamp_fusion), kind=kCustom, calls=%fused_computation.9.clone | custom fusion | bytes 1575936 | tf_op jit(solution)/shard_map/jit(_take)/gather | solution.py:87
  122.2 2.1 %gather_fusion.11 = f32[768,256]{1,0:T(8,128)S(1)} fusion(f32[256,256]{1,0:T(8,128)S(1)} %fusion.28, s32[1024]{0:T(1024)S(1)} %pad_clamp_fusion), kind=kCustom, calls=%fused_computation.11.clone | custom fusion | bytes 1575936 | tf_op jit(solution)/shard_map/jit(_take)/gather | solution.py:87
  (129 shorter events, 46.2 us)
Async XLA Ops:
  1.3 14.1 %all-to-all-start = ((bf16[16,4,1,256]{3,1,2,0:T(4,128)(2,1)}), bf16[16,4,1,256]{3,1,2,0:T(4,128)(2,1)S(1)}, u32[]{:S(2)}, u32[]{:S(2)}) async-start(bf16[16,4,1,256]{3,1,2,0:T(4,128)(2,1)} %stack.3), calls=%async_computation | async-start | bytes 65536 | tf_op jit(solution)/shard_map/all_to_all | solution.py:15
  15.4 5.3 %collective-permute-start = (f32[20,4,256]{2,1,0:T(4,128)S(1)}, f32[20,4,256]{2,1,0:T(4,128)S(1)}, u32[]{:S(2)}, u32[]{:S(2)}) collective-permute-start(f32[20,4,256]{2,1,0:T(4,128)S(1)} %get-tuple-element.30), channel_id=1, source_target_pairs={{0,1},{1,0},{2,3},{3,2},{4,5},{5,4},{6,7},{7,6},{8,9},{9,8},{10,11... | collective-permute-start | bytes 245768 | tf_op jit(solution)/shard_map/ppermute | solution.py:25
  17.0 4.6 %collective-permute-start.1 = (f32[20,4,256]{2,1,0:T(4,128)S(1)}, f32[20,4,256]{2,1,0:T(4,128)S(1)}, u32[]{:S(2)}, u32[]{:S(2)}) collective-permute-start(f32[20,4,256]{2,1,0:T(4,128)S(1)} %get-tuple-element.31), channel_id=1, source_target_pairs={{1,0},{0,1},{3,2},{2,3},{5,4},{4,5},{7,6},{6,7},{9,8},{8,9},{11,10... | collective-permute-start | bytes 245768 | tf_op jit(solution)/shard_map/ppermute | solution.py:27
  40.3 2.5 %copy-start.13 = (f32[21,256]{1,0:T(8,128)S(1)}, f32[21,256]{1,0:T(8,128)}, u32[]{:S(2)}) copy-start(f32[21,256]{1,0:T(8,128)} %get-tuple-element.44) | copy-start | bytes 64516
  40.4 6.8 %copy-start.7 = (f32[21,256]{0,1:T(8,128)S(1)}, f32[21,256]{0,1:T(8,128)}, u32[]{:S(2)}) copy-start(f32[21,256]{0,1:T(8,128)} %copy.54) | copy-start | bytes 64516
  47.2 4.8 %copy-start.3 = (f32[16,20,256]{1,0,2:T(8,128)S(1)}, f32[16,20,256]{1,0,2:T(8,128)}, u32[]{:S(2)}) copy-start(f32[16,20,256]{1,0,2:T(8,128)} %copy.77) | copy-start | bytes 983044
  52.6 1.3 %copy-start = (f32[16,20,256]{1,0,2:T(8,128)}, f32[16,20,256]{1,0,2:T(8,128)S(1)}, u32[]{:S(2)}) copy-start(f32[16,20,256]{1,0,2:T(8,128)S(1)} %fusion.21) | copy-start | bytes 983044
  54.0 1.7 %copy-start.9 = (f32[20,257]{1,0:T(8,128)S(1)}, f32[20,257]{1,0:T(8,128)}, u32[]{:S(2)}) copy-start(f32[20,257]{1,0:T(8,128)} %get-tuple-element.32) | copy-start | bytes 61684
  54.0 1.8 %copy-start.8 = (f32[20,257]{1,0:T(8,128)S(1)}, f32[20,257]{1,0:T(8,128)}, u32[]{:S(2)}) copy-start(f32[20,257]{1,0:T(8,128)} %get-tuple-element.33) | copy-start | bytes 61684
  54.0 1.9 %copy-start.14 = (pred[20,257]{1,0:T(8,128)(4,1)S(1)}, pred[20,257]{1,0:T(8,128)(4,1)}, u32[]{:S(2)}) copy-start(pred[20,257]{1,0:T(8,128)(4,1)} %get-tuple-element.18) | copy-start | bytes 15424
  54.0 2.1 %copy-start.5 = (f32[20,257]{0,1:T(8,128)S(1)}, f32[20,257]{0,1:T(8,128)}, u32[]{:S(2)}) copy-start(f32[20,257]{0,1:T(8,128)} %copy.62) | copy-start | bytes 61684
  54.0 2.1 %copy-start.19 = (pred[257]{0:T(512)(128)(4,1)S(1)}, pred[257]{0:T(512)(128)(4,1)}, u32[]{:S(2)}) copy-start(pred[257]{0:T(512)(128)(4,1)} %fusion.90) | copy-start | bytes 775
  56.1 6.4 %copy-start.1 = (f32[16,20,256]{1,0,2:T(8,128)S(1)}, f32[16,20,256]{1,0,2:T(8,128)}, u32[]{:S(2)}) copy-start(f32[16,20,256]{1,0,2:T(8,128)} %copy-done) | copy-start | bytes 983044
  63.4 2.0 %copy-start.2 = (f32[16,19,256]{1,0,2:T(8,128)}, f32[16,19,256]{1,0,2:T(8,128)S(1)}, u32[]{:S(2)}) copy-start(f32[16,19,256]{1,0,2:T(8,128)S(1)} %slice_subtract_fusion.4) | copy-start | bytes 933892
  63.4 2.0 %copy-start.12 = (f32[17,256]{1,0:T(8,128)S(1)}, f32[17,256]{1,0:T(8,128)}, u32[]{:S(2)}) copy-start(f32[17,256]{1,0:T(8,128)} %get-tuple-element.42) | copy-start | bytes 52228
  63.4 2.1 %copy-start.11 = (f32[17,256]{1,0:T(8,128)S(1)}, f32[17,256]{1,0:T(8,128)}, u32[]{:S(2)}) copy-start(f32[17,256]{1,0:T(8,128)} %get-tuple-element.43) | copy-start | bytes 52228
  63.4 2.2 %copy-start.15 = (pred[17,256]{1,0:T(8,128)(4,1)S(1)}, pred[17,256]{1,0:T(8,128)(4,1)}, u32[]{:S(2)}) copy-start(pred[17,256]{1,0:T(8,128)(4,1)} %get-tuple-element.16) | copy-start | bytes 13060
  63.4 2.3 %copy-start.6 = (f32[17,256]{0,1:T(8,128)S(1)}, f32[17,256]{0,1:T(8,128)}, u32[]{:S(2)}) copy-start(f32[17,256]{0,1:T(8,128)} %copy.66) | copy-start | bytes 52228
  72.3 0.9 copy-start.4
  76.4 5.6 %copy-start.17 = (s32[768]{0:T(1024)S(1)}, s32[768]{0:T(1024)}, u32[]{:S(2)}) copy-start(s32[768]{0:T(1024)} %get-tuple-element.47) | copy-start | bytes 9220
  76.4 5.6 %copy-start.16 = (s32[768]{0:T(1024)S(1)}, s32[768]{0:T(1024)}, u32[]{:S(2)}) copy-start(s32[768]{0:T(1024)} %get-tuple-element.46) | copy-start | bytes 9220
  76.4 5.6 %copy-start.18 = (s32[768,2]{0,1:T(2,128)S(1)}, s32[768,2]{0,1:T(2,128)}, u32[]{:S(2)}) copy-start(s32[768,2]{0,1:T(2,128)} %param.11) | copy-start | bytes 18436
  78.2 13.5 %all-to-all-start.1 = ((f32[16,16,1,256]{3,0,2,1:T(8,128)}), f32[16,16,1,256]{3,0,2,1:T(8,128)S(1)}, u32[]{:S(2)}, u32[]{:S(2)}) async-start(f32[16,16,1,256]{3,0,2,1:T(8,128)} %copy.74), calls=%async_computation.1 | async-start | bytes 524288 | tf_op jit(solution)/shard_map/all_to_all | solution.py:124
  93.9 2.1 %copy-start.20 = (f32[768]{0:T(1024)S(1)}, f32[768]{0:T(1024)}, u32[]{:S(2)}) copy-start(f32[768]{0:T(1024)} %param.9) | copy-start | bytes 9220
  (1 other events, 0.9 us)
